TPU v7x, 512 devices: a whole 4x8x8 slice. The times are simulated.
512 devices in a mesh: blk: 128 (over z, y, x_lo), rep: 4 (over x_hi, core).
Axes of the slice: x: 4 (x_hi: 2, x_lo: 2; x = x_hi * 2 + x_lo), y: 8, z: 8, core: 2. Of those that a mesh axis runs over, the one named last changes fastest.
Arguments:
- left_emb: float32 [32768, 256], P('blk'), may hold values from -6 to 6
- left_state: float32 [32768], P('blk'), may hold values from 0.3 to 30
- right_emb: float32 [32768, 256], P('blk'), may hold values from -8 to 8
- right_state: float32 [32768], P('blk'), may hold values from 0.3 to 30
- relation: float32 [2, 256, 256], replicated, may hold values from -0.375 to 0.375
- relation_state: float32 [2, 256, 256], replicated, may hold values from 5242.88 to 524288
- edge_src: int32 [128, 4, 2, 2, 512], P('blk', 'rep'), may hold values from 0 to 255
- edge_dst: int32 [128, 4, 2, 2, 512], P('blk', 'rep'), may hold values from 0 to 255
- edge_rel: int32 [128, 4, 2, 2, 512], P('blk', 'rep'), may hold values from 0 to 1
- negatives: int32 [128, 4, 2, 2, 512], P('blk', 'rep'), may hold values from 0 to 255
- batch_counts: int32 [128, 4, 2], P('blk', 'rep'), may hold values from 0 to 2, as said below
Outputs:
- left_new: float32 [32768, 256], P('blk')
- left_state_new: float32 [32768], P('blk')
- right_new: float32 [32768, 256], P('blk')
- right_state_new: float32 [32768], P('blk')
- relation_new: float32 [2, 256, 256], replicated
- relation_state_new: float32 [2, 256, 256], replicated
Inputs may be any that keep to these rules, and one draw needn't show every extreme that they name: `batch_counts`: in each bucket the live edge batches of the 4 devices of one blk index number at most 4; in every draw some bucket has exactly that many, with some device at 2.
All inputs are finite; a program needn't handle non-finite values.
Results may differ from a plain program's by a relative error of at most 0.035.
Values sent between devices are 32-bit elements; how exact they have to be, the bound alone decides.
No kernel may reach another device: no remote copies, remote signals or barrier semaphores. Data moves between devices by JAX's collectives and lax.ppermute only.
A program may use at most 64 MiB of HBM per device.

v0:
```python
import jax
import jax.numpy as jnp
from jax import lax
from jax.sharding import PartitionSpec as P

learn_rate = 0.1


def from_behind(block, axis, distance):
    devices = range(lax.axis_size(axis))
    route = [((i - distance) % len(devices), i) for i in devices]
    return lax.ppermute(block, axis, route)


def batch_terms(query_table, right_bf, src_row, dst_row, rel_row, neg_row, live_flag):
    queries = query_table[rel_row, src_row]
    pos_rows = right_bf[dst_row]
    neg_rows = right_bf[neg_row]
    pos_score = jnp.sum(queries.astype(jnp.float32) * pos_rows.astype(jnp.float32), axis=-1)
    neg_score = lax.dot_general(
        queries, neg_rows, (((1,), (1,)), ((), ())), preferred_element_type=jnp.float32
    )
    row_top = jnp.maximum(jnp.max(neg_score, axis=1), pos_score)
    pos_exp = jnp.exp(pos_score - row_top)
    neg_exp = jnp.exp(neg_score - row_top[:, None])
    row_total = pos_exp + jnp.sum(neg_exp, axis=1)
    pos_weight = (pos_exp / row_total - 1.0) * live_flag
    weights = (neg_exp / row_total[:, None] * live_flag).astype(jnp.bfloat16)
    query_grad = jnp.dot(weights, neg_rows, preferred_element_type=jnp.float32) + pos_weight[
        :, None
    ] * pos_rows.astype(jnp.float32)
    neg_grad = lax.dot_general(
        weights, queries, (((0,), (0,)), ((), ())), preferred_element_type=jnp.float32
    )
    pos_grad = pos_weight[:, None] * queries.astype(jnp.float32)
    return (query_grad, neg_grad, pos_grad)


def bucket_terms(left_rows, right_rows, operator_bf, sources, targets, relations, negs, live_flags):
    left_bf = left_rows.astype(jnp.bfloat16)
    right_bf = right_rows.astype(jnp.bfloat16)
    query_table = jnp.einsum(
        "nd,rkd->rnk", left_bf, operator_bf, preferred_element_type=jnp.float32
    ).astype(jnp.bfloat16)
    nrel, rows, width = query_table.shape

    def step(position, carry):
        table_grad, right_grad = carry
        src_row = lax.dynamic_index_in_dim(sources, position, 0, keepdims=False)
        dst_row = lax.dynamic_index_in_dim(targets, position, 0, keepdims=False)
        rel_row = lax.dynamic_index_in_dim(relations, position, 0, keepdims=False)
        neg_row = lax.dynamic_index_in_dim(negs, position, 0, keepdims=False)
        live_flag = lax.dynamic_index_in_dim(live_flags, position, 0, keepdims=False)
        query_grad, neg_grad, pos_grad = batch_terms(
            query_table, right_bf, src_row, dst_row, rel_row, neg_row, live_flag
        )
        table_grad = table_grad.at[rel_row, src_row].add(query_grad)
        right_grad = right_grad.at[neg_row].add(neg_grad).at[dst_row].add(pos_grad)
        return (table_grad, right_grad)

    start = (jnp.zeros((nrel, rows, width), jnp.float32), jnp.zeros((rows, width), jnp.float32))
    table_grad, right_grad = lax.fori_loop(0, sources.shape[0], step, start)
    table_bf = table_grad.astype(jnp.bfloat16)
    left_grad = jnp.einsum("rnk,rkd->nd", table_bf, operator_bf, preferred_element_type=jnp.float32)
    operator_grad = jnp.einsum("rnk,nd->rkd", table_bf, left_bf, preferred_element_type=jnp.float32)
    return (left_grad, right_grad, operator_grad)


def row_update(embedding, accum, gradient):
    accum_next = accum + jnp.mean(gradient * gradient, axis=-1)
    return (embedding - learn_rate * gradient / jnp.sqrt(accum_next)[:, None], accum_next)


def body(
    left_emb,
    left_state,
    right_emb,
    right_state,
    relation,
    relation_state,
    edge_src,
    edge_dst,
    edge_rel,
    negatives,
    batch_counts,
):
    operator_bf = relation.astype(jnp.bfloat16)
    nbatch = edge_src.shape[3]
    left_rows, left_accum = (left_emb, left_state)
    right_rows, right_accum = (right_emb, right_state)
    operator_total = jnp.zeros(relation.shape, jnp.float32)
    for bucket in range(2):
        sources = edge_src[0, 0, bucket]
        targets = edge_dst[0, 0, bucket]
        relations = edge_rel[0, 0, bucket]
        negs = negatives[0, 0, bucket]
        live_flags = (jnp.arange(nbatch) < batch_counts[0, 0, bucket]).astype(jnp.float32)
        left_grad, right_grad, operator_grad = bucket_terms(
            left_rows, right_rows, operator_bf, sources, targets, relations, negs, live_flags
        )
        operator_total = operator_total + lax.psum(operator_grad, ("blk", "rep"))
        left_sum, right_sum = lax.psum((left_grad, right_grad), "rep")
        left_rows, left_accum = row_update(left_rows, left_accum, left_sum)
        right_rows, right_accum = row_update(right_rows, right_accum, right_sum)
        if bucket == 0:
            left_rows, left_accum = from_behind((left_rows, left_accum), "blk", 1)
    relation_state_new = relation_state + operator_total * operator_total
    relation_new = relation - learn_rate * operator_total / jnp.sqrt(relation_state_new)
    return (left_rows, left_accum, right_rows, right_accum, relation_new, relation_state_new)


def solution(mesh):
    in_specs = (
        P("blk", None),
        P("blk"),
        P("blk", None),
        P("blk"),
        P(),
        P(),
        P("blk", "rep", None, None, None),
        P("blk", "rep", None, None, None),
        P("blk", "rep", None, None, None),
        P("blk", "rep", None, None, None),
        P("blk", "rep", None),
    )
    out_specs = (P("blk", None), P("blk"), P("blk", None), P("blk"), P(), P())
    return jax.shard_map(body, mesh=mesh, in_specs=in_specs, out_specs=out_specs, check_vma=False)
```

profile of v0, /device:TPU:1, one launch (start us, length us, event | category | flops | bytes accessed | tf_op | source)
XLA Modules:
  0.0 608.4 jit_solution(12801148130178979247)
XLA Ops:
  7.2 0.6 copy-done.23
  8.4 1.2 compare_convert_fusion.1
  9.6 1.0 convert_element_type.107
  10.6 1.1 convert_element_type.103
  14.1 91.3 %while.34 = (s32[]{:T(128)}, f32[2,256,256]{2,1,0:T(8,128)S(1)}, f32[256,256]{1,0:T(8,128)S(1)}, s32[2,512]{1,0:T(2,128)}, s32[2,512]{1,0:T(2,128)}, /*index=5*/...) while((s32[]{:T(128)}, f32[2,256,256]{2,1,0:T(8,128)S(1)}, ...), condition=%wide.region_7.8_spmd, body=%wide.region_0.7_spmd.sunk | while | flops 406075392 | bytes 12953801 | solution.py:62
  14.1 1.2 dynamic_slice.141
  15.3 0.7 compare_select_fusion.10
  16.0 0.7 or_select_fusion.4
  16.8 2.0 gather_fusion.1
  18.7 2.0 gather_fusion.2
  20.7 3.2 gather_fusion
  25.1 0.8 multiply_convert_fusion.4
  26.3 26.1 %scatter_fusion = f32[2,256,256]{2,1,0:T(8,128)S(1)} fusion(f32[2,256,256]{2,1,0:T(8,128)S(1)} %get-tuple-element.764, s32[512]{0:T(512)S(1)} %bitcast.154, f32[512,256]{1,0:T(8,128)S(1)} %convolution_add_fusion.5), kind=kCustom, calls=%fused_computation.6.clone.1 | custom fusion | flops 131072 | bytes 1576960 | tf_op jit(solution)/shard_map/while/body/eval_jaxpr/scatter-add | solution.py:57
  52.7 3.4 scatter_fusion.1
  56.1 3.6 scatter_custom_fusion.19
  59.7 1.2 dynamic_slice.141
  60.9 0.7 compare_select_fusion.10
  61.6 0.7 or_select_fusion.4
  62.4 2.0 gather_fusion.1
  64.4 2.0 gather_fusion.2
  66.3 3.2 gather_fusion
  70.8 0.8 multiply_convert_fusion.4
  71.9 26.1 %scatter_fusion = f32[2,256,256]{2,1,0:T(8,128)S(1)} fusion(f32[2,256,256]{2,1,0:T(8,128)S(1)} %get-tuple-element.764, s32[512]{0:T(512)S(1)} %bitcast.154, f32[512,256]{1,0:T(8,128)S(1)} %convolution_add_fusion.5), kind=kCustom, calls=%fused_computation.6.clone.1 | custom fusion | flops 131072 | bytes 1576960 | tf_op jit(solution)/shard_map/while/body/eval_jaxpr/scatter-add | solution.py:57
  98.3 3.4 scatter_fusion.1
  101.8 3.6 scatter_custom_fusion.19
  105.4 0.9 convolution_bitcast_fusion.1
  106.4 0.7 compare_convert_fusion
  107.0 1.1 fusion.16
  108.1 57.2 %all-reduce.10.cloned.1.call-done = (f32[256,256]{1,0:T(8,128)}, f32[256,256]{1,0:T(8,128)}) async-done(((f32[256,256]{1,0:T(8,128)}, f32[256,256]{1,0:T(8,128)}), (f32[256,256]{1,0:T(8,128)}, f32[256,256]{1,0:T(8,128)})) %all-reduce.10.cloned.1.call-update) | async-done | bytes 524304 | tf_op jit(solution)/shard_map/psum | solution.py:102
  165.3 1.1 multiply_reduce_fusion.2
  167.8 2.5 collective-permute-start
  170.9 11.4 %collective-permute-done = f32[256,256]{1,0:T(8,128)S(1)} collective-permute-done((f32[256,256]{1,0:T(8,128)S(1)}, f32[256,256]{1,0:T(8,128)S(1)}, u32[]{:S(2)}, u32[]{:S(2)}) %collective-permute-start) | collective-permute-done | bytes 262176 | tf_op jit(solution)/shard_map/ppermute | solution.py:12
  182.7 91.3 %while.35 = (s32[]{:T(128)}, f32[2,256,256]{2,1,0:T(8,128)S(1)}, f32[256,256]{1,0:T(8,128)S(1)}, s32[2,512]{1,0:T(2,128)}, s32[2,512]{1,0:T(2,128)}, /*index=5*/...) while((s32[]{:T(128)}, f32[2,256,256]{2,1,0:T(8,128)S(1)}, ...), condition=%wide.region_19.20_spmd, body=%wide.region_12.19_spmd.sunk | while | flops 406075392 | bytes 12921097 | solution.py:62
  183.8 0.7 compare_select_fusion.11
  184.5 0.7 or_select_fusion.5
  185.3 2.0 gather_fusion.4
  187.2 2.0 gather_fusion.5
  189.2 3.2 gather_fusion.3
  193.1 0.7 add_multiply_fusion.5
  193.7 0.8 multiply_convert_fusion.5
  194.9 26.1 %scatter_fusion.2 = f32[2,256,256]{2,1,0:T(8,128)S(1)} fusion(f32[2,256,256]{2,1,0:T(8,128)S(1)} %get-tuple-element.797, s32[512]{0:T(512)S(1)} %bitcast.155, f32[512,256]{1,0:T(8,128)S(1)} %convolution_add_fusion.6), kind=kCustom, calls=%fused_computation.9.clone.1 | custom fusion | flops 131072 | bytes 1576960 | tf_op jit(solution)/shard_map/while/body/eval_jaxpr/scatter-add | solution.py:57
  221.3 3.4 scatter_fusion.3
  224.8 3.6 scatter_custom_fusion.23
  229.5 0.7 compare_select_fusion.11
  230.2 0.7 or_select_fusion.5
  230.9 2.0 gather_fusion.4
  232.9 2.0 gather_fusion.5
  234.8 3.2 gather_fusion.3
  238.7 0.7 add_multiply_fusion.5
  239.4 0.8 multiply_convert_fusion.5
  240.6 26.1 %scatter_fusion.2 = f32[2,256,256]{2,1,0:T(8,128)S(1)} fusion(f32[2,256,256]{2,1,0:T(8,128)S(1)} %get-tuple-element.797, s32[512]{0:T(512)S(1)} %bitcast.155, f32[512,256]{1,0:T(8,128)S(1)} %convolution_add_fusion.6), kind=kCustom, calls=%fused_computation.9.clone.1 | custom fusion | flops 131072 | bytes 1576960 | tf_op jit(solution)/shard_map/while/body/eval_jaxpr/scatter-add | solution.py:57
  267.0 3.4 scatter_fusion.3
  270.5 3.6 scatter_custom_fusion.23
  274.1 2.2 convolution_add_fusion.2
  276.4 0.9 convolution_bitcast_fusion
  277.3 0.7 copy-done.25
  278.1 1.9 collective-permute-start.1
  280.0 262.9 %all-reduce.6.cloned.1.call-done = f32[2,256,256]{2,1,0:T(8,128)} async-done(((f32[2,256,256]{2,1,0:T(8,128)}), f32[2,256,256]{2,1,0:T(8,128)}) %all-reduce.6.cloned.1.call-update) | async-done | bytes 524304 | tf_op jit(solution)/shard_map/psum | solution.py:101
  542.9 2.2 multiply_subtract_fusion
  545.0 51.2 %all-reduce.8.cloned.1.call-done = (f32[256,256]{1,0:T(8,128)}, f32[256,256]{1,0:T(8,128)}) async-done(((f32[256,256]{1,0:T(8,128)}, f32[256,256]{1,0:T(8,128)}), (f32[256,256]{1,0:T(8,128)}, f32[256,256]{1,0:T(8,128)})) %all-reduce.8.cloned.1.call-update) | async-done | bytes 524304 | tf_op jit(solution)/shard_map/psum | solution.py:102
  596.2 1.1 multiply_reduce_fusion
  597.9 0.7 copy-done.16
  598.6 1.8 divide_subtract_fusion
  601.1 0.8 divide_subtract_fusion.1
  (122 shorter events, 15.3 us)
Async XLA Ops:
  7.2 158.1 %all-reduce.10.cloned.1.call-start = ((), (), s32[]{:S(2)}) async-start(), calls=%async_computation.2 | async-start | bytes 1048576 | tf_op jit(solution)/shard_map/psum | solution.py:102
  7.2 0.7 copy-start.23
  10.6 1.1 copy-start.2
  12.0 0.7 copy-start.17
  12.0 0.7 copy-start.18
  12.7 0.7 copy-start.19
  12.7 0.7 copy-start.20
  14.1 1.2 copy-start.11
  56.1 3.6 copy-start.12
  59.7 1.2 copy-start.11
  101.8 3.6 copy-start.12
  105.4 0.9 copy-start.1
  106.3 436.5 %all-reduce.6.cloned.1.call-start = ((), (), s32[]{:S(2)}) async-start(), calls=%async_computation | async-start | bytes 1048576 | tf_op jit(solution)/shard_map/psum | solution.py:101
  165.3 1.1 copy-start.9
  166.4 3.9 copy-start.13
  166.4 0.7 copy-start.24
  167.7 2.7 copy-start.21
  167.7 2.7 copy-start.3
  167.7 2.7 copy-start.5
  167.8 14.6 %collective-permute-start = (f32[256,256]{1,0:T(8,128)S(1)}, f32[256,256]{1,0:T(8,128)S(1)}, u32[]{:S(2)}, u32[]{:S(2)}) collective-permute-start(f32[256,256]{1,0:T(8,128)S(1)} %divide_subtract_fusion.3), channel_id=1, source_target_pairs={{508,0},{0,4},{4,8},{8,12},{12,16},{16,20},{20,24},{24,28},{28,32}... | collective-permute-start | bytes 786440 | tf_op jit(solution)/shard_map/ppermute | solution.py:12
  170.4 0.6 copy-start.15
  182.7 0.5 copy-start.26
  224.8 3.6 copy-start.27
  228.4 0.5 copy-start.26
  270.4 3.6 copy-start.27
  274.1 2.2 copy-start
  276.3 319.9 %all-reduce.8.cloned.1.call-start = ((), (), s32[]{:S(2)}) async-start(), calls=%async_computation.1 | async-start | bytes 1048576 | tf_op jit(solution)/shard_map/psum | solution.py:102
  276.4 266.5 %copy-start.10 = (f32[2,256,256]{2,1,0:T(8,128)S(1)}, f32[2,256,256]{2,1,0:T(8,128)}, u32[]{:S(2)}) copy-start(f32[2,256,256]{2,1,0:T(8,128)} %param.20) | copy-start | bytes 1572868
  277.3 265.6 %copy-start.7 = (f32[2,256,256]{2,1,0:T(8,128)S(1)}, f32[2,256,256]{2,1,0:T(8,128)}, u32[]{:S(2)}) copy-start(f32[2,256,256]{2,1,0:T(8,128)} %param.19) | copy-start | bytes 1572868
  277.3 0.7 copy-start.25
  278.1 322.5 %collective-permute-start.1 = (f32[256]{0:T(256)S(1)}, f32[256]{0:T(256)S(1)}, u32[]{:S(2)}, u32[]{:S(2)}) collective-permute-start(f32[256]{0:T(256)S(1)} %copy-done.25), channel_id=1, source_target_pairs={{508,0},{0,4},{4,8},{8,12},{12,16},{16,20},{20,24},{24,28},{28,32}... | collective-permute-start | bytes 3080 | tf_op jit(solution)/shard_map/ppermute | solution.py:12
  542.9 55.0 %copy-start.6 = (f32[256,256]{1,0:T(8,128)S(1)}, f32[256,256]{1,0:T(8,128)}, u32[]{:S(2)}) copy-start(f32[256,256]{1,0:T(8,128)} %get-tuple-element.559) | copy-start | bytes 786436
  545.0 52.9 %copy-start.4 = (f32[256,256]{1,0:T(8,128)S(1)}, f32[256,256]{1,0:T(8,128)}, u32[]{:S(2)}) copy-start(f32[256,256]{1,0:T(8,128)} %param.17) | copy-start | bytes 786436
  596.2 1.1 copy-start.14
  596.2 1.1 copy-start.22
  597.9 0.7 copy-start.16
  598.6 1.8 copy-start.8
Sparse Core Ops, SparseCore 0:
  106.5 58.7 all-reduce.9
  276.4 266.3 all-reduce.5
  546.7 49.4 all-reduce.7
where the time goes:
time: 609 us; the launch traced here: 608 us
  waiting for transfers between devices  383 us (63%)
  other arithmetic  158 us (26%)
  local copies, waits for them, and re-layouts  38.7 us (6%)
  between operations  14.1 us (2%)
  matrix products  9.56 us (2%)
    psum x1, waiting for transfers between devices, body(): operator_total = operator_total + lax.psum(operator_grad, ('blk', 'rep'))  263 us
    psum x2, waiting for transfers between devices, body(): left_sum, right_sum = lax.psum((left_grad, right_grad), 'rep')  108 us
    scatter-add x4, other arithmetic, step(): table_grad = table_grad.at[rel_row, src_row].add(query_grad)  104 us
    scatter-add x8, other arithmetic, step(): right_grad = right_grad.at[neg_row].add(neg_grad).at[dst_row].add(pos_grad)  28.1 us
    gather x4, local copies, waits for them, and re-layouts, batch_terms(): queries = query_table[rel_row, src_row]  12.7 us
  transfers between devices with their start and end apart: 5, of which 4 were waited for; matrix products, arithmetic and copies ran while one was open for 1% of the time, Pallas kernels for 0%

commit v1 on v0

--- a/solution.py
+++ b/solution.py
@@ -98,7 +98,7 @@
         left_grad, right_grad, operator_grad = bucket_terms(
             left_rows, right_rows, operator_bf, sources, targets, relations, negs, live_flags
         )
-        operator_total = operator_total + lax.psum(operator_grad, ("blk", "rep"))
+        operator_total = operator_total + lax.psum(lax.psum(operator_grad, "rep"), "blk")
         left_sum, right_sum = lax.psum((left_grad, right_grad), "rep")
         left_rows, left_accum = row_update(left_rows, left_accum, left_sum)
         right_rows, right_accum = row_update(right_rows, right_accum, right_sum)

time: 609 us -> 1430 us (2.35)
  the two profiles are of different devices: /device:TPU:1 before, /device:TPU:2 now
where the time goes in v1:
time: 1430 us
  waiting for transfers between devices  1200 us (84%)
  other arithmetic  156 us (11%)
  local copies, waits for them, and re-layouts  40.5 us (3%)
    psum x1, waiting for transfers between devices, body(): lax.psum(lax.psum(operator_grad, 'rep'), 'blk')  1090 us
    psum x2, waiting for transfers between devices, body(): left_sum, right_sum = lax.psum((left_grad, right_grad), 'rep')  106 us
    scatter-add x4, other arithmetic, step(): table_grad = table_grad.at[rel_row, src_row].add(query_grad)  104 us
  transfers between devices with their start and end apart: 5, of which 4 were waited for; matrix products, arithmetic and copies ran while one was open for 0% of the time, Pallas kernels for 0%

profile of v1, /device:TPU:2, one launch (start us, length us, event | category | flops | bytes accessed | tf_op | source)
XLA Modules:
  0.0 1429.7 jit_solution(7705722881691160842)
XLA Ops:
  7.2 0.6 copy-done.25
  8.4 1.2 compare_convert_fusion.1
  9.7 1.0 convert_element_type.107
  10.7 1.1 convert_element_type.103
  12.8 0.6 slice_bitcast_fusion.2
  14.2 91.4 %while.34 = (s32[]{:T(128)}, f32[2,256,256]{2,1,0:T(8,128)S(1)}, f32[256,256]{1,0:T(8,128)S(1)}, s32[2,512]{1,0:T(2,128)}, s32[2,512]{1,0:T(2,128)}, /*index=5*/...) while((s32[]{:T(128)}, f32[2,256,256]{2,1,0:T(8,128)S(1)}, ...), condition=%wide.region_7.8_spmd, body=%wide.region_0.7_spmd.sunk | while | flops 406075392 | bytes 12953801 | solution.py:62
  14.2 1.3 dynamic_slice.141
  15.5 0.7 compare_select_fusion.10
  16.2 0.7 or_select_fusion.4
  16.9 2.0 gather_fusion.1
  18.9 2.0 gather_fusion.2
  20.8 3.2 gather_fusion
  25.3 0.8 multiply_convert_fusion.4
  26.4 26.1 %scatter_fusion = f32[2,256,256]{2,1,0:T(8,128)S(1)} fusion(f32[2,256,256]{2,1,0:T(8,128)S(1)} %get-tuple-element.765, s32[512]{0:T(512)S(1)} %bitcast.154, f32[512,256]{1,0:T(8,128)S(1)} %convolution_add_fusion.5), kind=kCustom, calls=%fused_computation.6.clone.1 | custom fusion | flops 131072 | bytes 1576960 | tf_op jit(solution)/shard_map/while/body/eval_jaxpr/scatter-add | solution.py:57
  52.8 3.4 scatter_fusion.1
  56.3 3.6 scatter_custom_fusion.19
  59.9 1.3 dynamic_slice.141
  61.1 0.7 compare_select_fusion.10
  61.8 0.7 or_select_fusion.4
  62.6 2.0 gather_fusion.1
  64.6 2.0 gather_fusion.2
  66.5 3.2 gather_fusion
  71.0 0.8 multiply_convert_fusion.4
  72.1 26.1 %scatter_fusion = f32[2,256,256]{2,1,0:T(8,128)S(1)} fusion(f32[2,256,256]{2,1,0:T(8,128)S(1)} %get-tuple-element.765, s32[512]{0:T(512)S(1)} %bitcast.154, f32[512,256]{1,0:T(8,128)S(1)} %convolution_add_fusion.5), kind=kCustom, calls=%fused_computation.6.clone.1 | custom fusion | flops 131072 | bytes 1576960 | tf_op jit(solution)/shard_map/while/body/eval_jaxpr/scatter-add | solution.py:57
  98.5 3.4 scatter_fusion.1
  101.9 3.6 scatter_custom_fusion.19
  105.6 0.9 convolution_bitcast_fusion.1
  106.6 0.7 compare_convert_fusion
  107.2 1.1 fusion.16
  108.3 55.1 %all-reduce.10.cloned.1.call-done = (f32[256,256]{1,0:T(8,128)}, f32[256,256]{1,0:T(8,128)}) async-done(((f32[256,256]{1,0:T(8,128)}, f32[256,256]{1,0:T(8,128)}), (f32[256,256]{1,0:T(8,128)}, f32[256,256]{1,0:T(8,128)})) %all-reduce.10.cloned.1.call-update) | async-done | bytes 524304 | tf_op jit(solution)/shard_map/psum | solution.py:102
  163.4 1.1 multiply_reduce_fusion.2
  165.9 4.6 collective-permute-start
  171.1 5.3 collective-permute-done
  176.8 91.3 %while.35 = (s32[]{:T(128)}, f32[2,256,256]{2,1,0:T(8,128)S(1)}, f32[256,256]{1,0:T(8,128)S(1)}, s32[2,512]{1,0:T(2,128)}, s32[2,512]{1,0:T(2,128)}, /*index=5*/...) while((s32[]{:T(128)}, f32[2,256,256]{2,1,0:T(8,128)S(1)}, ...), condition=%wide.region_19.20_spmd, body=%wide.region_12.19_spmd.sunk | while | flops 406075392 | bytes 12921097 | solution.py:62
  177.9 0.7 compare_select_fusion.11
  178.6 0.7 or_select_fusion.5
  179.3 2.0 gather_fusion.4
  181.3 2.0 gather_fusion.5
  183.3 3.2 gather_fusion.3
  187.1 0.7 add_multiply_fusion.5
  187.8 0.8 multiply_convert_fusion.5
  189.0 26.1 %scatter_fusion.2 = f32[2,256,256]{2,1,0:T(8,128)S(1)} fusion(f32[2,256,256]{2,1,0:T(8,128)S(1)} %get-tuple-element.798, s32[512]{0:T(512)S(1)} %bitcast.155, f32[512,256]{1,0:T(8,128)S(1)} %convolution_add_fusion.6), kind=kCustom, calls=%fused_computation.9.clone.1 | custom fusion | flops 131072 | bytes 1576960 | tf_op jit(solution)/shard_map/while/body/eval_jaxpr/scatter-add | solution.py:57
  215.4 3.4 scatter_fusion.3
  218.9 3.6 scatter_custom_fusion.23
  223.6 0.7 compare_select_fusion.11
  224.3 0.7 or_select_fusion.5
  225.0 2.0 gather_fusion.4
  227.0 2.0 gather_fusion.5
  228.9 3.2 gather_fusion.3
  232.8 0.7 add_multiply_fusion.5
  233.5 0.8 multiply_convert_fusion.5
  234.7 26.1 %scatter_fusion.2 = f32[2,256,256]{2,1,0:T(8,128)S(1)} fusion(f32[2,256,256]{2,1,0:T(8,128)S(1)} %get-tuple-element.798, s32[512]{0:T(512)S(1)} %bitcast.155, f32[512,256]{1,0:T(8,128)S(1)} %convolution_add_fusion.6), kind=kCustom, calls=%fused_computation.9.clone.1 | custom fusion | flops 131072 | bytes 1576960 | tf_op jit(solution)/shard_map/while/body/eval_jaxpr/scatter-add | solution.py:57
  261.1 3.4 scatter_fusion.3
  264.5 3.6 scatter_custom_fusion.23
  268.2 0.9 convolution_bitcast_fusion
  269.3 1.1 convolution_add_fusion.2
  270.4 0.6 copy-done.27
  271.1 5.2 collective-permute-start.1
  276.3 51.4 %all-reduce.8.cloned.1.call-done = (f32[256,256]{1,0:T(8,128)}, f32[256,256]{1,0:T(8,128)}, f32[2,256,256]{2,1,0:T(8,128)}) async-done(((f32[256,256]{1,0:T(8,128)}, f32[256,256]{1,0:T(8,128)}, f32[2,256,256]{2,1,0:T(8,128)}), (f32[256,256]{1,0:T(8,128)}, f32[256,256]{1,0:T(8,128)}, f32[2,256,256]{2,1,0:T(8,128)})) %all-reduce.8.cloned.1.call-update) | async-done | bytes 1048592 | tf_op jit(solution)/shard_map/psum | solution.py:102
  327.7 0.9 copy-done.11
  330.6 0.8 divide_subtract_fusion.1
  332.1 0.9 divide_subtract_fusion
  332.9 1088.1 %all-reduce.6.cloned.1.call-done = f32[2,256,256]{2,1,0:T(8,128)} async-done(((f32[2,256,256]{2,1,0:T(8,128)}), f32[2,256,256]{2,1,0:T(8,128)}) %all-reduce.6.cloned.1.call-update) | async-done | bytes 524304 | tf_op jit(solution)/shard_map/psum | solution.py:101
  1421.0 2.1 multiply_subtract_fusion
  (126 shorter events, 16.3 us)
Async XLA Ops:
  7.2 156.2 %all-reduce.10.cloned.1.call-start = ((), (), s32[]{:S(2)}) async-start(), calls=%async_computation.2 | async-start | bytes 1048576 | tf_op jit(solution)/shard_map/psum | solution.py:102
  7.2 0.7 copy-start.25
  10.7 1.1 copy-start.2
  12.1 0.7 copy-start.19
  12.1 0.7 copy-start.20
  12.8 0.7 copy-start.21
  12.8 0.7 copy-start.22
  14.2 1.3 copy-start.13
  56.3 3.6 copy-start.14
  59.9 1.3 copy-start.13
  101.9 3.6 copy-start.14
  105.6 0.9 copy-start.1
  106.5 221.1 %all-reduce.8.cloned.1.call-start = ((), (), s32[]{:S(2)}) async-start(), calls=%async_computation.1 | async-start | bytes 2097152 | tf_op jit(solution)/shard_map/psum | solution.py:102
  163.4 1.1 copy-start.10
  164.5 6.0 copy-start.15
  164.5 0.7 copy-start.26
  165.8 4.7 copy-start.23
  165.8 4.8 copy-start.3
  165.8 4.8 copy-start.5
  165.9 10.6 collective-permute-start
  170.5 0.6 copy-start.17
  176.8 0.5 copy-start.28
  218.9 3.6 copy-start.29
  222.5 0.5 copy-start.28
  264.5 3.6 copy-start.29
  268.1 1.0 copy-start
  268.2 1.1 copy-start.8
  270.4 0.7 copy-start.27
  270.4 1150.6 %all-reduce.6.cloned.1.call-start = ((), (), s32[]{:S(2)}) async-start(), calls=%async_computation | async-start | bytes 1048576 | tf_op jit(solution)/shard_map/psum | solution.py:101
  271.1 58.9 %collective-permute-start.1 = (f32[256]{0:T(256)S(1)}, f32[256]{0:T(256)S(1)}, u32[]{:S(2)}, u32[]{:S(2)}) collective-permute-start(f32[256]{0:T(256)S(1)} %copy-done.27), channel_id=1, source_target_pairs={{508,0},{0,4},{4,8},{8,12},{12,16},{16,20},{20,24},{24,28},{28,32}... | collective-permute-start | bytes 3080 | tf_op jit(solution)/shard_map/ppermute | solution.py:12
  327.6 0.9 copy-start.11
  327.7 2.2 copy-start.9
  328.6 0.7 copy-start.16
  328.6 0.7 copy-start.24
  330.5 0.9 copy-start.4
  330.6 1.1 copy-start.6
  331.4 0.7 copy-start.18
  332.1 1088.9 %copy-start.7 = (f32[2,256,256]{2,1,0:T(8,128)S(1)}, f32[2,256,256]{2,1,0:T(8,128)}, u32[]{:S(2)}) copy-start(f32[2,256,256]{2,1,0:T(8,128)} %param.19) | copy-start | bytes 1572868
  332.1 1088.9 %copy-start.12 = (f32[2,256,256]{2,1,0:T(8,128)S(1)}, f32[2,256,256]{2,1,0:T(8,128)}, u32[]{:S(2)}) copy-start(f32[2,256,256]{2,1,0:T(8,128)} %param.20) | copy-start | bytes 1572868
Sparse Core Ops, SparseCore 0:
  106.6 56.6 all-reduce.9
  270.5 57.0 all-reduce.7
  330.8 1090.1 all-reduce.5
